TPU v7x, 32 devices: a whole 2x2x4 slice. The times are simulated.
32 devices in a mesh: groups: 2 (over x), step: 2 (over core), person: 8 (over z, y).
Axes of the slice: x: 2, y: 2, z: 4, core: 2. Of those that a mesh axis runs over, the one named last changes fastest.
Arguments:
- chain: float32 [8, 128, 4, 512], P(('groups', 'step'), 'person'), parts along dimension 0, may hold values from -6 to 6
- start: float32 [256, 4, 512], P(('groups', 'person')), parts along dimension 0, may hold values from -6 to 6
- noise: bfloat16 [8, 128, 4, 512], P(('groups', 'step'), 'person'), parts along dimension 0, may hold values from -6 to 6
- timesteps: int32 [8], P(('groups', 'step')), parts along dimension 0, may hold values from 1 to 1000
- rates: float32 [8], P(('groups', 'step')), parts along dimension 0, may hold values from 0.05 to 0.5
- noise_scales: float32 [8], P(('groups', 'step')), parts along dimension 0, may hold values from 0.1 to 0.5
- time_weight: bfloat16 [512, 512], replicated, may hold values from -0.25 to 0.25
- w_query: bfloat16 [2, 512, 512], replicated, may hold values from -1.75 to 1.75
- w_keyval: bfloat16 [2, 512, 1024], replicated, may hold values from -0.25 to 0.25
- w_attn_out: bfloat16 [2, 512, 512], replicated, may hold values from -0.25 to 0.25
- w_up: bfloat16 [2, 512, 1024], replicated, may hold values from -0.25 to 0.25
- w_down: bfloat16 [2, 1024, 512], replicated, may hold values from -0.1875 to 0.1875
- gains: float32 [2, 2, 512], replicated, may hold values from 0.1 to 1.9
- final_gain: float32 [512], replicated, may hold values from 0.1 to 1.9
- w_output: bfloat16 [512, 512], replicated, may hold values from -0.25 to 0.25
Outputs:
- new_chain: float32 [8, 128, 4, 512], P(('groups', 'step'), 'person'), parts along dimension 0
There are 2 independent parts, one for each index of `groups`. A program takes and returns all parts, laid end to end along the dimension named above; an argument that names none is the same for every part. Nothing has to cross between parts.
All inputs are finite; a program needn't handle non-finite values.
Results may differ from a plain program's by a relative error of at most 0.004.
Values may be sent and summed in bfloat16 or wider, within the bound.
A program may use at most 64 MiB of HBM per device.

v0:
```python
import functools
import math

import jax
import jax.numpy as jnp
from jax import lax
from jax.sharding import PartitionSpec as P

HEADS = 8


def shifted(block, axis, distance):
    devices = range(lax.axis_size(axis))
    route = [(i - distance, i) for i in devices if i - distance in devices]
    return lax.ppermute(block, axis, route)


def prefix(array, axis, combine, identity):
    peers, here = (lax.axis_size(axis), lax.axis_index(axis))
    everything = lax.all_gather(array, axis)
    start = jnp.broadcast_to(jnp.asarray(identity, array.dtype), array.shape)

    def hop(k, before):
        reached = k < here
        new = combine(before, everything[k])
        return jnp.where(reached, new, before)

    return lax.fori_loop(0, peers, hop, start)


def time_features(timesteps, feature_width):
    half_width = feature_width // 2
    freqs = jnp.exp(-math.log(10000.0) * jnp.arange(half_width).astype(jnp.float32) / half_width)
    angles = timesteps.astype(jnp.float32)[:, None] * freqs[None, :]
    return jnp.concatenate([jnp.sin(angles), jnp.cos(angles)], axis=1)


def rms_norm(values, gain):
    return values * lax.rsqrt(jnp.mean(values * values, axis=-1, keepdims=True) + 1e-06) * gain


def project_rows(piece_rows, offset, weight):
    return jnp.einsum("srd,de->sre", piece_rows, weight, preferred_element_type=jnp.float32).astype(
        jnp.bfloat16
    )


def add_terms(earlier, later):
    return earlier + later


def attend(queries, keyval, head_count):
    steps_here, row_count, feature_width = queries.shape
    key_count = keyval.shape[1]
    head_dim = feature_width // head_count
    q_heads = queries.reshape(steps_here, row_count, head_count, head_dim)
    k_heads = keyval[:, :, :feature_width].reshape(steps_here, key_count, head_count, head_dim)
    v_heads = keyval[:, :, feature_width:].reshape(steps_here, key_count, head_count, head_dim)
    scores = jnp.einsum(
        "sqhd,skhd->shqk", q_heads, k_heads, preferred_element_type=jnp.float32
    ) / math.sqrt(head_dim)
    expo = jnp.exp(30.0 * jnp.tanh(scores / 30.0))
    weights = (expo / jnp.sum(expo, axis=-1, keepdims=True)).astype(jnp.bfloat16)
    attended = jnp.einsum("shqk,skhd->sqhd", weights, v_heads, preferred_element_type=jnp.float32)
    return attended.reshape(steps_here, row_count, feature_width).astype(jnp.bfloat16)


def local(
    chain,
    start,
    noise,
    timesteps,
    rates,
    noise_scales,
    time_weight,
    w_query,
    w_keyval,
    w_attn_out,
    w_up,
    w_down,
    gains,
    final_gain,
    w_output,
):
    steps_here, persons, tokens, feature_width = chain.shape
    row_count = persons * tokens
    arrived = shifted(chain[-1], "step", 1)
    is_first = lax.axis_index("step") == 0
    earlier = jnp.where(is_first, start, arrived)
    points = jnp.concatenate([earlier[None], chain[:-1]], axis=0).reshape(
        steps_here, row_count, feature_width
    )
    embedded = time_features(timesteps, feature_width).astype(jnp.bfloat16)
    temb = jax.nn.silu(jnp.dot(embedded, time_weight, preferred_element_type=jnp.float32))
    hidden = points + temb[:, None, :]
    for layer_index in range(w_query.shape[0]):
        normed = rms_norm(hidden, gains[layer_index, 0]).astype(jnp.bfloat16)
        queries = jnp.einsum(
            "srd,de->sre", normed, w_query[layer_index], preferred_element_type=jnp.float32
        ).astype(jnp.bfloat16)
        projector = functools.partial(project_rows, weight=w_keyval[layer_index])
        keyval = projector(lax.all_gather(normed, "person", axis=1, tiled=True), jnp.int32(0))
        attended = attend(queries, keyval, HEADS)
        hidden = hidden + jnp.einsum(
            "srd,de->sre", attended, w_attn_out[layer_index], preferred_element_type=jnp.float32
        )
        mixed = rms_norm(hidden, gains[layer_index, 1]).astype(jnp.bfloat16)
        upward = jax.nn.gelu(
            jnp.einsum("srd,df->srf", mixed, w_up[layer_index], preferred_element_type=jnp.float32)
        ).astype(jnp.bfloat16)
        hidden = hidden + jnp.einsum(
            "srf,fd->srd", upward, w_down[layer_index], preferred_element_type=jnp.float32
        )
    final_rows = rms_norm(hidden, final_gain).astype(jnp.bfloat16)
    predicted = jnp.einsum("srd,de->sre", final_rows, w_output, preferred_element_type=jnp.float32)
    noise_rows = noise.reshape(steps_here, row_count, feature_width).astype(jnp.float32)
    drift = rates[:, None, None] * (predicted - points) + noise_scales[:, None, None] * noise_rows
    running = jnp.cumsum(drift, axis=0)
    totals = running[-1]
    before = prefix(totals, "step", add_terms, jnp.zeros_like(totals))
    new_chain = start.reshape(row_count, feature_width)[None] + (before[None] + running)
    return new_chain.reshape(steps_here, persons, tokens, feature_width)


def solution(mesh):
    placed = (
        P(("groups", "step"), "person", None, None),
        P(("groups", "person"), None, None),
        P(("groups", "step"), "person", None, None),
        P(("groups", "step")),
        P(("groups", "step")),
        P(("groups", "step")),
        P(),
        P(),
        P(),
        P(),
        P(),
        P(),
        P(),
        P(),
        P(),
    )
    return jax.shard_map(
        local,
        mesh=mesh,
        in_specs=placed,
        out_specs=P(("groups", "step"), "person", None, None),
        check_vma=False,
    )
```

profile of v0, /device:TPU:0, one launch (start us, length us, event | category | flops | bytes accessed | tf_op | source)
XLA Modules:
  0.0 139.0 jit_solution(9981813758981660182)
XLA Ops:
  6.5 1.1 fusion.96
  7.6 2.4 %collective-permute-start = (f32[16,4,512]{2,1,0:T(4,128)S(1)}, f32[16,4,512]{2,1,0:T(4,128)S(1)}, u32[]{:S(2)}, u32[]{:S(2)}) collective-permute-start(f32[16,4,512]{2,1,0:T(4,128)S(1)} %get-tuple-element.113), channel_id=1, source_target_pairs={{0,8},{1,9},{2,10},{3,11},{4,12},{5,13},{6,14},{7,15},{16,24},{17,... | collective-permute-start | bytes 393224 | tf_op jit(solution)/shard_map/ppermute | solution.py:15
  10.9 1.2 divide_multiply_fusion
  12.9 0.9 broadcast_select_fusion
  14.9 1.1 convolution_convert_fusion.5
  16.2 41.0 %all-gather.3.cloned.1.call-done = bf16[2,512,512]{2,1,0:T(8,128)(2,1)} async-done(((bf16[2,64,512]{2,1,0:T(8,128)(2,1)}), bf16[2,512,512]{2,1,0:T(8,128)(2,1)}) %all-gather.3.cloned.1.call-update) | async-done | bytes 1048592 | tf_op jit(solution)/shard_map/all_gather | solution.py:102
  57.3 2.8 %convolution_convert_fusion.1 = bf16[2,512,1024]{2,1,0:T(8,128)(2,1)S(1)} fusion(bf16[2,512,512]{2,1,0:T(8,128)(2,1)} %all-gather.3.cloned.1.call-done, bf16[2,512,1024]{2,1,0:T(8,128)(2,1)} %param.25), kind=kOutput, calls=%fused_computation.6 | convolution fusion | flops 1074790400 | bytes 4194304 | tf_op jit(solution)/shard_map/srd,de->sre/dot_general | solution.py:43
  60.1 1.2 fusion.95
  61.3 1.5 %copy.33 = bf16[2,512,512]{1,2,0:T(8,128)(2,1)S(1)} copy(bf16[2,512,512]{2,1,0:T(8,128)(2,1)} %get-tuple-element.110) | data formatting | bytes 2097152 | tf_op jit(solution)/shard_map/slice | solution.py:57
  62.8 1.3 copy.32
  64.1 2.0 %multiply_exponential_fusion.1 = f32[2,8,64,512]{3,2,1,0:T(8,128)} fusion(bf16[2,512,8,64]{1,3,2,0:T(8,128)(2,1)S(1)} %bitcast.108, bf16[2,64,8,64]{3,2,1,0:T(8,128)(2,1)S(1)} %reshape.91), kind=kOutput, calls=%fused_computation.4 | convolution fusion | flops 68157440 | bytes 3276800 | tf_op jit(solution)/shard_map/sqhd,skhd->shqk/dot_general | solution.py:59
  66.1 2.8 %convolution_convert_fusion.3 = bf16[2,8,64,64]{3,2,1,0:T(8,128)(2,1)S(1)} fusion(bf16[2,512,8,64]{1,3,2,0:T(8,128)(2,1)S(1)} %bitcast.111, f32[2,8,64,512]{3,2,1,0:T(8,128)} %multiply_exponential_fusion.1), kind=kOutput, calls=%fused_computation.8 | convolution fusion | flops 68224512 | bytes 3276800 | tf_op jit(solution)/shard_map/shqk,skhd->sqhd/dot_general | solution.py:64
  69.3 2.3 %multiply_reduce_fusion.2 = (f32[2,64]{1,0:T(2,128)S(1)}, f32[2,64,512]{2,1,0:T(8,128)S(1)}) fusion(f32[2,64,512]{2,1,0:T(8,128)S(1)} %get-tuple-element.121, bf16[2,1024,512]{2,1,0:T(8,128)(2,1)} %param.28, bf16[2,512,1024]{2,1,0:T(8,128)(2,1)} %param.27, f32[512]{0:T(512)S(1)} %bitcast.123, f32[2,64]{1,0:T(2,128)S(1)} %add_rsqrt_fusion.3), kind=kOutput, calls=%fused_computation.69 | convolution fusion | flops 270008192 | bytes 2887168 | tf_op jit(solution)/shard_map/srf,fd->srd/dot_general | solution.py:111
  72.4 1.3 convolution_convert_fusion.4
  74.7 36.8 %all-gather.5.cloned.1.call-done = bf16[2,512,512]{2,1,0:T(8,128)(2,1)} async-done(((bf16[2,64,512]{2,1,0:T(8,128)(2,1)}), bf16[2,512,512]{2,1,0:T(8,128)(2,1)}) %all-gather.5.cloned.1.call-update) | async-done | bytes 1048592 | tf_op jit(solution)/shard_map/all_gather | solution.py:102
  111.5 2.8 %convolution_convert_fusion = bf16[2,512,1024]{2,1,0:T(8,128)(2,1)S(1)} fusion(bf16[2,512,512]{2,1,0:T(8,128)(2,1)} %all-gather.5.cloned.1.call-done, bf16[2,512,1024]{2,1,0:T(8,128)(2,1)} %param.25), kind=kOutput, calls=%fused_computation.5 | convolution fusion | flops 1074790400 | bytes 4194304 | tf_op jit(solution)/shard_map/srd,de->sre/dot_general | solution.py:43
  114.3 1.2 fusion.94
  115.5 1.5 %copy.37 = bf16[2,512,512]{1,2,0:T(8,128)(2,1)S(1)} copy(bf16[2,512,512]{2,1,0:T(8,128)(2,1)} %get-tuple-element.108) | data formatting | bytes 2097152 | tf_op jit(solution)/shard_map/slice | solution.py:57
  117.0 1.3 copy.36
  118.3 3.1 %multiply_exponential_fusion = f32[2,8,64,512]{3,2,1,0:T(8,128)} fusion(bf16[2,512,8,64]{1,3,2,0:T(8,128)(2,1)S(1)} %bitcast.109, bf16[2,64,8,64]{3,2,1,0:T(8,128)(2,1)} %reshape.94), kind=kOutput, calls=%fused_computation.2 | convolution fusion | flops 68157440 | bytes 3276800 | tf_op jit(solution)/shard_map/sqhd,skhd->shqk/dot_general | solution.py:59
  121.4 3.5 %convolution_convert_fusion.2 = bf16[2,8,64,64]{3,2,1,0:T(8,128)(2,1)} fusion(bf16[2,512,8,64]{1,3,2,0:T(8,128)(2,1)S(1)} %bitcast.112, f32[2,8,64,512]{3,2,1,0:T(8,128)} %multiply_exponential_fusion), kind=kOutput, calls=%fused_computation.7 | convolution fusion | flops 68224512 | bytes 3276800 | tf_op jit(solution)/shard_map/shqk,skhd->sqhd/dot_general | solution.py:64
  124.9 1.3 multiply_reduce_fusion.1
  126.3 2.2 %multiply_reduce_fusion = (f32[2,64]{1,0:T(2,128)S(1)}, f32[2,64,512]{2,1,0:T(8,128)S(1)}) fusion(f32[2,64,512]{2,1,0:T(8,128)S(1)} %get-tuple-element.125, bf16[2,1024,512]{2,1,0:T(8,128)(2,1)} %param.28, bf16[2,512,1024]{2,1,0:T(8,128)(2,1)} %param.27, f32[512]{0:T(512)S(1)} %bitcast.122, f32[2,64]{1,0:T(2,128)S(1)} %add_rsqrt_fusion.1), kind=kOutput, calls=%fused_computation.65 | convolution fusion | flops 270008192 | bytes 2887168 | tf_op jit(solution)/shard_map/srf,fd->srd/dot_general | solution.py:111
  129.2 2.0 %all_gather.11 = f32[2,64,512]{2,1,0:T(8,128)S(1)} all-gather(f32[1,64,512]{2,1,0:T(8,128)S(1)} %slice.88), channel_id=1, replica_groups=mesh['groups'=2,'step'=2,'person'=8] {'step'}, dimensions={0}, use_global_device_ids=true | all-gather | bytes 393216 | tf_op jit(solution)/shard_map/all_gather | solution.py:20
  (57 shorter events, 6.5 us)
Async XLA Ops:
  6.5 122.0 %copy-start = (bf16[512,512]{1,0:T(8,128)(2,1)S(1)}, bf16[512,512]{1,0:T(8,128)(2,1)}, u32[]{:S(2)}) copy-start(bf16[512,512]{1,0:T(8,128)(2,1)} %param.31) | copy-start | bytes 1572868
  6.5 8.4 %copy-start.10 = (bf16[2,512,512]{2,1,0:T(8,128)(2,1)S(1)}, bf16[2,512,512]{2,1,0:T(8,128)(2,1)}, u32[]{:S(2)}) copy-start(bf16[2,512,512]{2,1,0:T(8,128)(2,1)} %param.24) | copy-start | bytes 3145732
  6.5 50.7 %all-gather.3.cloned.1.call-start = ((), (), s32[]{:S(2)}) async-start(), calls=%async_computation | async-start | bytes 1179648 | tf_op jit(solution)/shard_map/all_gather | solution.py:102
  7.6 5.3 %collective-permute-start = (f32[16,4,512]{2,1,0:T(4,128)S(1)}, f32[16,4,512]{2,1,0:T(4,128)S(1)}, u32[]{:S(2)}, u32[]{:S(2)}) collective-permute-start(f32[16,4,512]{2,1,0:T(4,128)S(1)} %get-tuple-element.113), channel_id=1, source_target_pairs={{0,8},{1,9},{2,10},{3,11},{4,12},{5,13},{6,14},{7,15},{16,24},{17,... | collective-permute-start | bytes 393224 | tf_op jit(solution)/shard_map/ppermute | solution.py:15
  14.8 96.6 %all-gather.5.cloned.1.call-start = ((), (), s32[]{:S(2)}) async-start(), calls=%async_computation.1 | async-start | bytes 1179648 | tf_op jit(solution)/shard_map/all_gather | solution.py:102
  64.1 2.0 %copy-start.3 = (bf16[2,512,512]{1,2,0:T(8,128)(2,1)S(1)}, bf16[2,512,512]{1,2,0:T(8,128)(2,1)}, u32[]{:S(2)}) copy-start(bf16[2,512,512]{1,2,0:T(8,128)(2,1)} %copy.32) | copy-start | bytes 3145732
  66.1 2.8 %copy-start.1 = (bf16[2,512,512]{2,1,0:T(8,128)(2,1)S(1)}, bf16[2,512,512]{2,1,0:T(8,128)(2,1)}, u32[]{:S(2)}) copy-start(bf16[2,512,512]{2,1,0:T(8,128)(2,1)} %param.26) | copy-start | bytes 3145732
  69.3 3.1 %copy-start.6 = (bf16[2,16,4,512]{3,2,1,0:T(4,128)(2,1)S(1)}, bf16[2,16,4,512]{3,2,1,0:T(4,128)(2,1)}, u32[]{:S(2)}) copy-start(bf16[2,16,4,512]{3,2,1,0:T(4,128)(2,1)} %param.19) | copy-start | bytes 393220
  118.3 3.1 %copy-start.4 = (bf16[2,512,512]{1,2,0:T(8,128)(2,1)S(1)}, bf16[2,512,512]{1,2,0:T(8,128)(2,1)}, u32[]{:S(2)}) copy-start(bf16[2,512,512]{1,2,0:T(8,128)(2,1)} %copy.36) | copy-start | bytes 3145732
  121.4 3.5 %copy-start.2 = (bf16[2,512,512]{2,1,0:T(8,128)(2,1)S(1)}, bf16[2,512,512]{2,1,0:T(8,128)(2,1)}, u32[]{:S(2)}) copy-start(bf16[2,512,512]{2,1,0:T(8,128)(2,1)} %param.26) | copy-start | bytes 3145732
  126.2 2.3 %copy-start.7 = (f32[512]{0:T(512)S(1)}, f32[512]{0:T(512)}, u32[]{:S(2)}) copy-start(f32[512]{0:T(512)} %param.30) | copy-start | bytes 6148
  126.2 2.3 %copy-start.8 = (f32[2]{0:T(128)S(1)}, f32[2]{0:T(128)}, u32[]{:S(2)}) copy-start(f32[2]{0:T(128)} %param.22) | copy-start | bytes 28
  126.3 2.3 %copy-start.9 = (f32[2]{0:T(128)S(1)}, f32[2]{0:T(128)}, u32[]{:S(2)}) copy-start(f32[2]{0:T(128)} %param.21) | copy-start | bytes 28
  128.9 2.5 %copy-start.5 = (f32[16,4,512]{2,1,0:T(4,128)S(1)}, f32[16,4,512]{2,1,0:T(4,128)}, u32[]{:S(2)}) copy-start(f32[16,4,512]{2,1,0:T(4,128)} %param.18) | copy-start | bytes 393220
Sparse Core Ops, SparseCore 0:
  15.0 42.2 all-gather.2
  72.5 38.9 all-gather.4
where the time goes:
time: 139 us
  waiting for transfers between devices  77.9 us (56%)
  matrix products  27.2 us (20%)
  between operations  13.7 us (10%)
  local copies, waits for them, and re-layouts  11.3 us (8%)
  other arithmetic  4.43 us (3%)
  starting transfers between devices  2.41 us (2%)
  blocking collectives  1.99 us (1%)
    all_gather x2, waiting for transfers between devices, local(): lax.all_gather(normed, 'person', axis=1, tiled=True)  77.8 us
    dot_general x2, matrix products, attend(): jnp.einsum('shqk,skhd->sqhd', weights, v_heads, preferred_element_type=jn...  6.36 us
    dot_general x2, matrix products, project_rows(): jnp.einsum('srd,de->sre', piece_rows, weight, preferred_element_type=jnp....  5.58 us
    slice x4, local copies, waits for them, and re-layouts, attend(): keyval[:, :, :feature_width]  5.34 us
    dot_general x2, matrix products, attend(): jnp.einsum('sqhd,skhd->shqk', q_heads, k_heads, preferred_element_type=jn...  5.09 us
    dot_general x2, matrix products, local(): jnp.einsum('srf,fd->srd', upward, w_down[layer_index], preferred_element_...  4.51 us
  transfers between devices with their start and end apart: 3, of which 2 were waited for; matrix products, arithmetic and copies ran while one was open for 5% of the time, Pallas kernels for 0%

commit v1 on v0

v1 whole, which is shorter than its diff:
```python
import functools
import math

import jax
import jax.numpy as jnp
from jax import lax
from jax.experimental import pallas as pl
from jax.experimental.pallas import tpu as pltpu
from jax.sharding import PartitionSpec as P

HEADS = 8
MESH = pl.DeviceIdType.MESH
BF = jnp.bfloat16
F32 = jnp.float32


def dot(a, b):
    return jnp.dot(a, b, preferred_element_type=F32)


def rms_norm(values, gain):
    return values * lax.rsqrt(jnp.mean(values * values, axis=-1, keepdims=True) + 1e-06) * gain


def kernel(
    sizes,
    chain_ref, start_ref, noise_ref, times_ref, rates_ref, scales_ref,
    tw_ref, wq_ref, wkv_ref, wo_ref, wu_ref, wd_ref, gains_ref, fgain_ref, wout_ref,
    out_ref,
    chain_v, start_v, noise_v, tw_v, wq_v, wkv_v, wo_v, wu_v, wd_v, wout_v,
    send_v, recv_v, temb_v, prev_v, gath, pout, pin, tot_out, tot_in,
    load_sem, ssend, srecv, tsend, trecv, vsend, vrecv, gsend, grecv, nsend, nrecv, fsend, frecv,
    rsend, rrecv, usend, urecv,
):
    n, cores, h, rows, width, layers = sizes
    window = h * cores
    teams = n // window
    mine = h * rows
    me_p, me_s = lax.axis_index("person"), lax.axis_index("step")
    spot, j = me_p // teams, me_p % teams

    def device(person, step):
        return {"person": person, "step": step}

    def remote(src, dst, send_sem, recv_sem, person, step):
        return pltpu.make_async_remote_copy(
            src_ref=src, dst_ref=dst, send_sem=send_sem, recv_sem=recv_sem,
            device_id=device(person, step), device_id_type=MESH,
        )

    loads = {}

    def load(name, src, dst):
        copy = pltpu.make_async_copy(src, dst, load_sem.at[len(loads)])
        loads[name] = copy
        copy.start()

    load("chain", chain_ref, chain_v)
    load("start", start_ref, start_v)
    load("tw", tw_ref, tw_v)
    for l in range(layers):
        load(("wq", l), wq_ref.at[l], wq_v.at[l])
        load(("wkv", l), wkv_ref.at[l], wkv_v.at[l])
        load(("wo", l), wo_ref.at[l], wo_v.at[l])
        load(("wu", l), wu_ref.at[l], wu_v.at[l])
        load(("wd", l), wd_ref.at[l], wd_v.at[l])
    load("wout", wout_ref, wout_v)
    load("noise", noise_ref, noise_v)

    barrier = pltpu.get_barrier_semaphore()
    for dq in range(window):
        for ds in range(cores):
            if dq or ds:
                pl.semaphore_signal(
                    barrier, inc=1,
                    device_id=device(((spot + dq) % window) * teams + j, (me_s + ds) % cores),
                    device_id_type=MESH,
                )
    for d in range(1, teams):
        pl.semaphore_signal(
            barrier, inc=1, device_id=device(spot * teams + (j + d) % teams, me_s), device_id_type=MESH
        )

    loads["chain"].wait()
    loads["start"].wait()
    is_last = me_s == cores - 1
    for t in range(h):
        block = chain_v[t].reshape(rows, width)
        if t == h - 1:
            block = jnp.where(is_last, start_v[...].reshape(rows, width), block)
        send_v[t] = block.astype(BF)
    pl.semaphore_wait(barrier, window * cores - 1 + teams - 1)

    scatter = []
    for t in range(h):
        position = (me_s * h + t + 1) % window
        to_p, to_s, slot = position * teams + j, spot // h, spot % h
        own = (to_p == me_p) & (to_s == me_s)
        copy = remote(send_v.at[t], recv_v.at[slot], ssend.at[t], srecv.at[slot], to_p, to_s)
        scatter.append((own, copy))

        @pl.when(jnp.logical_not(own))
        def _():
            copy.start()

        @pl.when(own)
        def _():
            recv_v[slot] = send_v[t]

    hand = remote(chain_v.at[h - 1], prev_v, vsend.at[0], vrecv.at[0], me_p, (me_s + 1) % cores)

    @pl.when(me_s < cores - 1)
    def _():
        hand.start()

    lane = lax.broadcasted_iota(jnp.int32, (8, width), 1)
    sub = lax.broadcasted_iota(jnp.int32, (8, width), 0)
    half = width // 2
    index = jnp.where(lane < half, lane, lane - half).astype(F32)
    freqs = jnp.exp(-math.log(10000.0) * index / half)
    when = jnp.zeros((8, width), F32)
    for t in range(h):
        when = jnp.where(sub == t, times_ref[t].astype(F32), when)
    angles = when * freqs
    features = jnp.where(lane < half, jnp.sin(angles), jnp.cos(angles)).astype(BF)
    loads["tw"].wait()
    temb = dot(features, tw_v[...])
    temb_v[me_s] = temb * (1.0 / (1.0 + jnp.exp(-temb)))
    shares = []
    for d in range(1, cores):
        share = remote(
            temb_v.at[me_s], temb_v.at[me_s], tsend.at[d - 1], trecv.at[d - 1], me_p, (me_s + d) % cores
        )
        share.start()
        shares.append(share)
    for d in range(1, cores):
        other = (me_s + cores - d) % cores
        remote(temb_v.at[other], temb_v.at[other], tsend.at[d - 1], trecv.at[d - 1], me_p, other).wait_recv()
    time_row = temb_v[spot // h, pl.ds(spot % h, 1), :]

    from_s = ((spot + window - 1) % window) // h
    for b in range(h):
        own = (me_s * h + b == spot) & (from_s == me_s)

        @pl.when(jnp.logical_not(own))
        def _():
            remote(
                recv_v.at[b], recv_v.at[b], ssend.at[0], srecv.at[b], me_p, (me_s + 1) % cores
            ).wait_recv()

    hidden = recv_v[...].reshape(mine, width).astype(F32) + time_row

    head_dim = width // HEADS
    wide = min(256, width)
    per = wide // head_dim
    groups = width // wide
    lane_head = lax.broadcasted_iota(jnp.int32, (mine, wide), 1) // head_dim
    masks = [lane_head == i for i in range(per)]
    inner = 1.0 / (math.sqrt(head_dim) * 30.0)
    outer = 30.0 * math.log2(math.e)
    sends = []

    for l in range(layers):
        normed = rms_norm(hidden, gains_ref[2 * l : 2 * l + 1, :]).astype(BF)
        gath[l, j, me_s] = normed
        own_block = gath.at[l, j, me_s]
        for d in range(1, teams):
            copy = remote(
                own_block, own_block, gsend.at[l, d - 1], grecv.at[l, d - 1],
                spot * teams + (j + d) % teams, me_s,
            )
            copy.start()
            sends.append(copy)
        for e in range(1, cores):
            copy = remote(
                own_block, own_block, nsend.at[l, e - 1], nrecv.at[l, e - 1], me_p, (me_s + e) % cores
            )
            copy.start()
            sends.append(copy)
        loads["wq", l].wait()
        queries = dot(normed, wq_v[l]).astype(BF)
        stacked = []
        for g in range(groups):
            piece = queries[:, g * wide : (g + 1) * wide]
            stacked.append(jnp.concatenate([jnp.where(m, piece, jnp.zeros_like(piece)) for m in masks], axis=0))
        loads["wkv", l].wait()

        def round_of(team, carry, l=l, stacked=stacked):
            sums, dens = carry
            keyval = dot(gath[l, team].reshape(cores * mine, width), wkv_v[l]).astype(BF)
            new_sums, new_dens = [], []
            for g in range(groups):
                keys = keyval[:, g * wide : (g + 1) * wide]
                values = keyval[:, width + g * wide : width + (g + 1) * wide]
                scores = lax.dot_general(
                    stacked[g], keys, (((1,), (1,)), ((), ())), preferred_element_type=F32
                )
                expo = jnp.exp2(jnp.tanh(scores * inner) * outer)
                part = dot(expo.astype(BF), values)
                total = sums[g]
                for i in range(per):
                    total = total + jnp.where(masks[i], part[i * mine : (i + 1) * mine], 0.0)
                new_sums.append(total)
                den = dens[g]
                for c in range(0, cores * mine, 128):
                    den = den + expo[:, c : c + 128]
                new_dens.append(den)
            return tuple(new_sums), tuple(new_dens)

        carry = (
            tuple(jnp.zeros((mine, wide), F32) for _ in range(groups)),
            tuple(jnp.zeros((per * mine, 128), F32) for _ in range(groups)),
        )
        for e in range(1, cores):
            other = gath.at[l, j, (me_s + cores - e) % cores]
            remote(
                other, other, nsend.at[l, e - 1], nrecv.at[l, e - 1], me_p, (me_s + e) % cores
            ).wait_recv()
        carry = round_of(j, carry)
        for d in range(1, teams):
            team = (j + teams - d) % teams
            block = gath.at[l, team, me_s]
            remote(
                block, block, gsend.at[l, d - 1], grecv.at[l, d - 1], spot * teams + team, me_s
            ).wait_recv()
            for e in range(1, cores):
                copy = remote(
                    block, block, fsend.at[l, d - 1, e - 1], frecv.at[l, d - 1, e - 1],
                    me_p, (me_s + e) % cores,
                )
                copy.start()
                sends.append(copy)
        for d in range(1, teams):
            team = (j + teams - d) % teams
            for e in range(1, cores):
                block = gath.at[l, team, (me_s + cores - e) % cores]
                remote(
                    block, block, fsend.at[l, d - 1, e - 1], frecv.at[l, d - 1, e - 1],
                    me_p, (me_s + e) % cores,
                ).wait_recv()
        if teams <= 2:
            for d in range(1, teams):
                carry = round_of((j + teams - d) % teams, carry)
        else:
            carry = lax.fori_loop(1, teams, lambda d, c: round_of((j + teams - d) % teams, c), carry)
        sums, dens = carry
        pieces = []
        for g in range(groups):
            inverse = 1.0 / jnp.sum(dens[g], axis=-1, keepdims=True)
            scale = jnp.zeros((mine, wide), F32)
            for i in range(per):
                scale = jnp.where(masks[i], inverse[i * mine : (i + 1) * mine], scale)
            pieces.append((sums[g] * scale).astype(BF))
        attended = jnp.concatenate(pieces, axis=1)
        loads["wo", l].wait()
        hidden = hidden + dot(attended, wo_v[l])
        mixed = rms_norm(hidden, gains_ref[2 * l + 1 : 2 * l + 2, :]).astype(BF)
        loads["wu", l].wait()
        upward = jax.nn.gelu(dot(mixed, wu_v[l])).astype(BF)
        loads["wd", l].wait()
        hidden = hidden + dot(upward, wd_v[l])

    final_rows = rms_norm(hidden, fgain_ref[...]).astype(BF)
    loads["wout"].wait()
    predicted = dot(final_rows, wout_v[...]).astype(BF)

    returns = []
    for b in range(h):
        pout[b] = predicted[b * rows : (b + 1) * rows]
        to_p, to_s, slot = (me_s * h + b) * teams + j, spot // h, spot % h
        own = (to_p == me_p) & (to_s == me_s)
        copy = remote(pout.at[b], pin.at[slot], rsend.at[b], rrecv.at[slot], to_p, to_s)
        returns.append((own, copy))

        @pl.when(jnp.logical_not(own))
        def _():
            copy.start()

        @pl.when(own)
        def _():
            pin[slot] = pout[b]

    @pl.when(me_s > 0)
    def _():
        remote(prev_v, prev_v, vsend.at[0], vrecv.at[0], me_p, (me_s + 1) % cores).wait_recv()

    @pl.when(me_s == 0)
    def _():
        prev_v[...] = start_v[...]

    loads["noise"].wait()
    first = start_v[...].reshape(rows, width)
    bases = []
    total = jnp.zeros((rows, width), F32)
    for t in range(h):
        points = (prev_v[...] if t == 0 else chain_v[t - 1]).reshape(rows, width)
        noise = noise_v[t].astype(F32).reshape(rows, width)
        total = total + (scales_ref[t] * noise - rates_ref[t] * points)
        bases.append(total)
    running = jnp.zeros((rows, width), F32)
    sums = []
    for t in range(h):
        own = ((me_s * h + t) * teams + j == me_p) & (spot // h == me_s)

        @pl.when(jnp.logical_not(own))
        def _():
            remote(
                pin.at[t], pin.at[t], rsend.at[0], rrecv.at[t], me_p, (me_s + 1) % cores
            ).wait_recv()

        running = running + rates_ref[t] * pin[t].astype(F32)
        sums.append(bases[t] + running)
    tot_out[...] = sums[-1]
    ups = []
    for d in range(1, cores):
        up = remote(tot_out, tot_in.at[d - 1], usend.at[d - 1], urecv.at[d - 1], me_p, (me_s + d) % cores)
        ups.append(up)

        @pl.when(me_s + d < cores)
        def _():
            up.start()

    for d in range(1, cores):

        @pl.when(me_s - d >= 0)
        def _():
            remote(
                tot_in.at[d - 1], tot_in.at[d - 1], usend.at[d - 1], urecv.at[d - 1],
                me_p, (me_s + cores - d) % cores,
            ).wait_recv()

    before = first
    for d in range(1, cores):
        before = before + jnp.where(me_s - d >= 0, tot_in[d - 1], 0.0)
    for t in range(h):
        out_ref[t] = (before + sums[t]).reshape(out_ref.shape[1:])

    for own, copy in scatter + returns:

        @pl.when(jnp.logical_not(own))
        def _():
            copy.wait_send()

    @pl.when(me_s < cores - 1)
    def _():
        hand.wait_send()

    for copy in shares + sends:
        copy.wait_send()
    for d, up in enumerate(ups):

        @pl.when(me_s + d + 1 < cores)
        def _():
            up.wait_send()


def local(n, cores, chain, start, noise, timesteps, rates, noise_scales, time_weight, w_query, w_keyval,
          w_attn_out, w_up, w_down, gains, final_gain, w_output):
    h, persons, tokens, width = chain.shape
    rows = persons * tokens
    layers = w_query.shape[0]
    teams = n // (h * cores)
    mine = h * rows
    sizes = (n, cores, h, rows, width, layers)
    any_spec = pl.BlockSpec(memory_space=pl.ANY)
    smem = pl.BlockSpec(memory_space=pltpu.SMEM)
    vmem = pl.BlockSpec(memory_space=pltpu.VMEM)
    dma = pltpu.SemaphoreType.DMA
    peers, teamed = max(cores - 1, 1), max(teams - 1, 1)
    scratch = [
        pltpu.VMEM(chain.shape, F32), pltpu.VMEM(start.shape, F32), pltpu.VMEM(noise.shape, BF),
        pltpu.VMEM(time_weight.shape, BF), pltpu.VMEM(w_query.shape, BF), pltpu.VMEM(w_keyval.shape, BF),
        pltpu.VMEM(w_attn_out.shape, BF), pltpu.VMEM(w_up.shape, BF), pltpu.VMEM(w_down.shape, BF),
        pltpu.VMEM(w_output.shape, BF),
        pltpu.VMEM((h, rows, width), BF), pltpu.VMEM((h, rows, width), BF),
        pltpu.VMEM((cores, 8, width), F32), pltpu.VMEM(start.shape, F32),
        pltpu.VMEM((layers, teams, cores, mine, width), BF),
        pltpu.VMEM((h, rows, width), BF), pltpu.VMEM((h, rows, width), BF),
        pltpu.VMEM((rows, width), F32), pltpu.VMEM((peers, rows, width), F32),
        dma((5 + 5 * layers,)), dma((h,)), dma((h,)), dma((peers,)), dma((peers,)), dma((1,)), dma((1,)),
        dma((layers, teamed)), dma((layers, teamed)), dma((layers, peers)), dma((layers, peers)),
        dma((layers, teamed, peers)), dma((layers, teamed, peers)),
        dma((h,)), dma((h,)), dma((peers,)), dma((peers,)),
    ]
    return pl.pallas_call(
        functools.partial(kernel, sizes),
        out_shape=jax.ShapeDtypeStruct(chain.shape, F32),
        in_specs=[any_spec] * 3 + [smem] * 3 + [any_spec] * 6 + [vmem] * 2 + [any_spec],
        out_specs=vmem,
        scratch_shapes=scratch,
        compiler_params=pltpu.CompilerParams(
            collective_id=0, has_side_effects=True, vmem_limit_bytes=48 * 1024 * 1024
        ),
    )(
        chain, start, noise, timesteps, rates, noise_scales, time_weight, w_query, w_keyval, w_attn_out,
        w_up, w_down, gains.reshape(-1, width), final_gain.reshape(1, width), w_output,
    )


def solution(mesh):
    placed = (
        P(("groups", "step"), "person", None, None),
        P(("groups", "person"), None, None),
        P(("groups", "step"), "person", None, None),
        P(("groups", "step")),
        P(("groups", "step")),
        P(("groups", "step")),
    ) + (P(),) * 9
    return jax.shard_map(
        functools.partial(local, mesh.shape["person"], mesh.shape["step"]),
        mesh=mesh,
        in_specs=placed,
        out_specs=P(("groups", "step"), "person", None, None),
        check_vma=False,
    )
```

time: 139 us -> 44.4 us (0.32)
  waiting for transfers between devices: 77.9 us -> 0 us
  Pallas kernels: 0 us -> 31 us
  matrix products: 27.2 us -> 0 us
  between operations: 13.7 us -> 0.02 us
  other arithmetic: 4.43 us -> 0 us
  starting transfers between devices: 2.41 us -> 0 us
  blocking collectives: 1.99 us -> 0 us
  local copies, waits for them, and re-layouts: 11.3 us -> 12.9 us
    all_gather x2 -> x0, waiting for transfers between devices: 77.8 us -> none  [local(): lax.all_gather(normed, 'person', axis=1, tiled=True)]
    pallas_call x0 -> x1, Pallas kernels: none -> 31 us  [local(): pl.pallas_call(functools.partial(kernel, sizes), out_shape=jax.ShapeDtype...]
    dot_general x14 -> x0, matrix products: 27.2 us -> none  [the longest x2 6.36 us: attend(): jnp.einsum('shqk,skhd->sqhd', weights, v_heads, preferred_element_type=jn...]
    unnamed x23 -> x25, local copies, waits for them, and re-layouts: 0.06 us -> 12.2 us
    slice x9 -> x0, local copies, waits for them, and re-layouts: 9.91 us -> none  [the longest x4 5.34 us: attend(): keyval[:, :, :feature_width]]
    ppermute x1 -> x0, starting transfers between devices: 2.36 us -> none  [shifted(): return lax.ppermute(block, axis, route)]
    convert_element_type x3 -> x0, other arithmetic: 2.17 us -> none  [the longest x2 1.51 us: local(): normed = rms_norm(hidden, gains[layer_index, 0]).astype(jnp.bfloat16)]
    all_gather x1 -> x0, blocking collectives: 1.99 us -> none  [prefix(): everything = lax.all_gather(array, axis)]
  transfers between devices with their start and end apart: 3 -> 0, of which waited for: 2 -> 0; matrix products, arithmetic and copies ran while one was open for 5% -> 0% of each run, Pallas kernels for 0% -> 0%
where the time goes in v1:
time: 44.4 us; the launch traced here: 43.9 us
  Pallas kernels  31 us (70%)
  local copies, waits for them, and re-layouts  12.9 us (29%)
    pallas_call x1, Pallas kernels, local(): pl.pallas_call(functools.partial(kernel, sizes), out_shape=jax.ShapeDtype...  31 us
    unnamed x25, local copies, waits for them, and re-layouts  12.2 us

profile of v1, /device:TPU:0, one launch (start us, length us, event | category | flops | bytes accessed | tf_op | source)
XLA Modules:
  0.0 43.9 jit_solution(9580519575054067582)
XLA Ops:
  0.0 0.7 %reshape.6.gains_ref = f32[4,512]{1,0:T(4,128)S(1)} reshape(f32[2,2,512]{2,1,0:T(2,128)} %param.27) | data formatting | bytes 16384 | tf_op jit(solution)/shard_map/reshape | solution.py:396
  0.7 0.0 copy-start
  0.7 1.6 %copy-done = bf16[2,512,1024]{2,1,0:T(8,128)(2,1)S(1)} copy-done((bf16[2,512,1024]{2,1,0:T(8,128)(2,1)S(1)}, bf16[2,512,1024]{2,1,0:T(8,128)(2,1)}, u32[]{:S(2)}) %copy-start) | copy-done | bytes 2097176
  2.3 0.0 copy-start.1
  2.3 1.2 %copy-done.1 = bf16[2,512,512]{2,1,0:T(8,128)(2,1)S(1)} copy-done((bf16[2,512,512]{2,1,0:T(8,128)(2,1)S(1)}, bf16[2,512,512]{2,1,0:T(8,128)(2,1)}, u32[]{:S(2)}) %copy-start.1) | copy-done | bytes 1048600
  3.5 0.0 copy-start.2
  3.5 1.2 %copy-done.2 = bf16[2,512,512]{2,1,0:T(8,128)(2,1)S(1)} copy-done((bf16[2,512,512]{2,1,0:T(8,128)(2,1)S(1)}, bf16[2,512,512]{2,1,0:T(8,128)(2,1)}, u32[]{:S(2)}) %copy-start.2) | copy-done | bytes 1048600
  4.8 1.0 %copy-done.3 = bf16[512,512]{1,0:T(8,128)(2,1)S(1)} copy-done((bf16[512,512]{1,0:T(8,128)(2,1)S(1)}, bf16[512,512]{1,0:T(8,128)(2,1)}, u32[]{:S(2)}) %copy-start.3) | copy-done | bytes 524312
  5.8 0.0 copy-start.4
  5.8 1.0 %copy-done.4 = bf16[512,512]{1,0:T(8,128)(2,1)S(1)} copy-done((bf16[512,512]{1,0:T(8,128)(2,1)S(1)}, bf16[512,512]{1,0:T(8,128)(2,1)}, u32[]{:S(2)}) %copy-start.4) | copy-done | bytes 524312
  6.8 0.0 copy-start.5
  6.8 0.9 %copy-done.5 = f32[2,16,4,512]{3,2,1,0:T(4,128)S(1)} copy-done((f32[2,16,4,512]{3,2,1,0:T(4,128)S(1)}, f32[2,16,4,512]{3,2,1,0:T(4,128)}, u32[]{:S(2)}) %copy-start.5) | copy-done | bytes 262168
  7.8 0.0 copy-start.6
  7.8 0.9 %copy-done.6 = f32[16,4,512]{2,1,0:T(4,128)S(1)} copy-done((f32[16,4,512]{2,1,0:T(4,128)S(1)}, f32[16,4,512]{2,1,0:T(4,128)}, u32[]{:S(2)}) %copy-start.6) | copy-done | bytes 131096
  8.7 0.0 copy-start.7
  8.7 0.9 %copy-done.7 = bf16[2,16,4,512]{3,2,1,0:T(4,128)(2,1)S(1)} copy-done((bf16[2,16,4,512]{3,2,1,0:T(4,128)(2,1)S(1)}, bf16[2,16,4,512]{3,2,1,0:T(4,128)(2,1)}, u32[]{:S(2)}) %copy-start.7) | copy-done | bytes 131096
  9.6 0.0 copy-start.8
  9.6 0.7 %copy-done.8 = f32[512]{0:T(512)S(1)} copy-done((f32[512]{0:T(512)S(1)}, f32[512]{0:T(512)}, u32[]{:S(2)}) %copy-start.8) | copy-done | bytes 2072
  10.3 0.0 copy-start.9
  10.3 0.7 %copy-done.9 = s32[2]{0:T(128)S(1)} copy-done((s32[2]{0:T(128)S(1)}, s32[2]{0:T(128)}, u32[]{:S(2)}) %copy-start.9) | copy-done | bytes 32
  10.9 0.7 %copy-done.10 = f32[2]{0:T(128)S(1)} copy-done((f32[2]{0:T(128)S(1)}, f32[2]{0:T(128)}, u32[]{:S(2)}) %copy-start.10) | copy-done | bytes 32
  11.6 0.7 %copy-done.11 = f32[2]{0:T(128)S(1)} copy-done((f32[2]{0:T(128)S(1)}, f32[2]{0:T(128)}, u32[]{:S(2)}) %copy-start.11) | copy-done | bytes 32
  12.2 31.0 %shard_map.145 = f32[2,16,4,512]{3,2,1,0:T(4,128)S(1)} custom-call(f32[2,16,4,512]{3,2,1,0:T(4,128)S(1)} %copy-done.5, f32[16,4,512]{2,1,0:T(4,128)S(1)} %copy-done.6, bf16[2,16,4,512]{3,2,1,0:T(4,128)(2,1)S(1)} %copy-done.7, s32[2]{0:T(128)S(1)} %copy-done.9, f32[2]{0:T(128)S(1)} %copy-done.10, f32[2]{0:T(128)S(1)} %copy-done.11, ...), custom_call_target="tpu_custom_call" | custom-call | tf_op jit(solution)/shard_map/pallas_call | solution.py:385
  43.2 0.7 %copy.17 = f32[2,16,4,512]{3,2,1,0:T(4,128)} copy(f32[2,16,4,512]{3,2,1,0:T(4,128)S(1)} %shard_map.145) | data formatting | bytes 524288
  (3 shorter events, 0.0 us)
Async XLA Ops:
  0.7 1.6 %copy-start = (bf16[2,512,1024]{2,1,0:T(8,128)(2,1)S(1)}, bf16[2,512,1024]{2,1,0:T(8,128)(2,1)}, u32[]{:S(2)}) copy-start(bf16[2,512,1024]{2,1,0:T(8,128)(2,1)} %wkv_ref.1) | copy-start | bytes 6291460
  2.3 1.2 %copy-start.1 = (bf16[2,512,512]{2,1,0:T(8,128)(2,1)S(1)}, bf16[2,512,512]{2,1,0:T(8,128)(2,1)}, u32[]{:S(2)}) copy-start(bf16[2,512,512]{2,1,0:T(8,128)(2,1)} %wq_ref.1) | copy-start | bytes 3145732
  3.5 1.2 %copy-start.2 = (bf16[2,512,512]{2,1,0:T(8,128)(2,1)S(1)}, bf16[2,512,512]{2,1,0:T(8,128)(2,1)}, u32[]{:S(2)}) copy-start(bf16[2,512,512]{2,1,0:T(8,128)(2,1)} %wo_ref.1) | copy-start | bytes 3145732
  4.8 1.0 %copy-start.3 = (bf16[512,512]{1,0:T(8,128)(2,1)S(1)}, bf16[512,512]{1,0:T(8,128)(2,1)}, u32[]{:S(2)}) copy-start(bf16[512,512]{1,0:T(8,128)(2,1)} %tw_ref.1) | copy-start | bytes 1572868
  5.8 1.0 %copy-start.4 = (bf16[512,512]{1,0:T(8,128)(2,1)S(1)}, bf16[512,512]{1,0:T(8,128)(2,1)}, u32[]{:S(2)}) copy-start(bf16[512,512]{1,0:T(8,128)(2,1)} %wout_ref.1) | copy-start | bytes 1572868
  6.8 0.9 %copy-start.5 = (f32[2,16,4,512]{3,2,1,0:T(4,128)S(1)}, f32[2,16,4,512]{3,2,1,0:T(4,128)}, u32[]{:S(2)}) copy-start(f32[2,16,4,512]{3,2,1,0:T(4,128)} %chain_ref.1) | copy-start | bytes 786436
  7.8 0.9 %copy-start.6 = (f32[16,4,512]{2,1,0:T(4,128)S(1)}, f32[16,4,512]{2,1,0:T(4,128)}, u32[]{:S(2)}) copy-start(f32[16,4,512]{2,1,0:T(4,128)} %start_ref.1) | copy-start | bytes 393220
  8.7 0.9 %copy-start.7 = (bf16[2,16,4,512]{3,2,1,0:T(4,128)(2,1)S(1)}, bf16[2,16,4,512]{3,2,1,0:T(4,128)(2,1)}, u32[]{:S(2)}) copy-start(bf16[2,16,4,512]{3,2,1,0:T(4,128)(2,1)} %noise_ref.1) | copy-start | bytes 393220
  9.6 0.7 %copy-start.8 = (f32[512]{0:T(512)S(1)}, f32[512]{0:T(512)}, u32[]{:S(2)}) copy-start(f32[512]{0:T(512)} %param.28) | copy-start | bytes 6148
  10.3 0.7 %copy-start.9 = (s32[2]{0:T(128)S(1)}, s32[2]{0:T(128)}, u32[]{:S(2)}) copy-start(s32[2]{0:T(128)} %times_ref.1) | copy-start | bytes 28
  10.9 0.7 %copy-start.10 = (f32[2]{0:T(128)S(1)}, f32[2]{0:T(128)}, u32[]{:S(2)}) copy-start(f32[2]{0:T(128)} %rates_ref.1) | copy-start | bytes 28
  11.6 0.7 %copy-start.11 = (f32[2]{0:T(128)S(1)}, f32[2]{0:T(128)}, u32[]{:S(2)}) copy-start(f32[2]{0:T(128)} %scales_ref.1) | copy-start | bytes 28

commit v2 on v1

--- a/solution.py
+++ b/solution.py
@@ -24,10 +24,10 @@
 
 def kernel(
     sizes,
-    chain_ref, start_ref, noise_ref, times_ref, rates_ref, scales_ref,
-    tw_ref, wq_ref, wkv_ref, wo_ref, wu_ref, wd_ref, gains_ref, fgain_ref, wout_ref,
+    chain_ref, start_ref, noise_ref, times_hbm, rates_hbm, scales_hbm,
+    tw_ref, wq_ref, wkv_ref, wo_ref, wu_ref, wd_ref, gains_hbm, fgain_hbm, wout_ref,
     out_ref,
-    chain_v, start_v, noise_v, tw_v, wq_v, wkv_v, wo_v, wu_v, wd_v, wout_v,
+    times_ref, rates_ref, scales_ref, gains_ref, fgain_ref, chain_v, start_v, noise_v, tw_v, wq_v, wkv_v, wo_v, wu_v, wd_v, wout_v,
     send_v, recv_v, temb_v, prev_v, gath, pout, pin, tot_out, tot_in,
     load_sem, ssend, srecv, tsend, trecv, vsend, vrecv, gsend, grecv, nsend, nrecv, fsend, frecv,
     rsend, rrecv, usend, urecv,
@@ -57,7 +57,9 @@
 
     load("chain", chain_ref, chain_v)
     load("start", start_ref, start_v)
+    load("times", times_hbm, times_ref)
     load("tw", tw_ref, tw_v)
+    load("gains", gains_hbm, gains_ref)
     for l in range(layers):
         load(("wq", l), wq_ref.at[l], wq_v.at[l])
         load(("wkv", l), wkv_ref.at[l], wkv_v.at[l])
@@ -66,6 +68,9 @@
         load(("wd", l), wd_ref.at[l], wd_v.at[l])
     load("wout", wout_ref, wout_v)
     load("noise", noise_ref, noise_v)
+    load("fgain", fgain_hbm, fgain_ref)
+    load("rates", rates_hbm, rates_ref)
+    load("scales", scales_hbm, scales_ref)
 
     barrier = pltpu.get_barrier_semaphore()
     for dq in range(window):
@@ -119,6 +124,7 @@
     index = jnp.where(lane < half, lane, lane - half).astype(F32)
     freqs = jnp.exp(-math.log(10000.0) * index / half)
     when = jnp.zeros((8, width), F32)
+    loads["times"].wait()
     for t in range(h):
         when = jnp.where(sub == t, times_ref[t].astype(F32), when)
     angles = when * freqs
@@ -160,8 +166,9 @@
     outer = 30.0 * math.log2(math.e)
     sends = []
 
+    loads["gains"].wait()
     for l in range(layers):
-        normed = rms_norm(hidden, gains_ref[2 * l : 2 * l + 1, :]).astype(BF)
+        normed = rms_norm(hidden, gains_ref[l, 0:1, :]).astype(BF)
         gath[l, j, me_s] = normed
         own_block = gath.at[l, j, me_s]
         for d in range(1, teams):
@@ -254,13 +261,14 @@
         attended = jnp.concatenate(pieces, axis=1)
         loads["wo", l].wait()
         hidden = hidden + dot(attended, wo_v[l])
-        mixed = rms_norm(hidden, gains_ref[2 * l + 1 : 2 * l + 2, :]).astype(BF)
+        mixed = rms_norm(hidden, gains_ref[l, 1:2, :]).astype(BF)
         loads["wu", l].wait()
         upward = jax.nn.gelu(dot(mixed, wu_v[l])).astype(BF)
         loads["wd", l].wait()
         hidden = hidden + dot(upward, wd_v[l])
 
-    final_rows = rms_norm(hidden, fgain_ref[...]).astype(BF)
+    loads["fgain"].wait()
+    final_rows = rms_norm(hidden, fgain_ref[...].reshape(1, width)).astype(BF)
     loads["wout"].wait()
     predicted = dot(final_rows, wout_v[...]).astype(BF)
 
@@ -289,6 +297,8 @@
         prev_v[...] = start_v[...]
 
     loads["noise"].wait()
+    loads["rates"].wait()
+    loads["scales"].wait()
     first = start_v[...].reshape(rows, width)
     bases = []
     total = jnp.zeros((rows, width), F32)
@@ -362,12 +372,13 @@
     teams = n // (h * cores)
     mine = h * rows
     sizes = (n, cores, h, rows, width, layers)
-    any_spec = pl.BlockSpec(memory_space=pl.ANY)
-    smem = pl.BlockSpec(memory_space=pltpu.SMEM)
+    hbm = pl.BlockSpec(memory_space=pltpu.HBM)
     vmem = pl.BlockSpec(memory_space=pltpu.VMEM)
     dma = pltpu.SemaphoreType.DMA
     peers, teamed = max(cores - 1, 1), max(teams - 1, 1)
     scratch = [
+        pltpu.SMEM(timesteps.shape, jnp.int32), pltpu.SMEM(rates.shape, F32), pltpu.SMEM(rates.shape, F32),
+        pltpu.VMEM(gains.shape, F32), pltpu.VMEM(final_gain.shape, F32),
         pltpu.VMEM(chain.shape, F32), pltpu.VMEM(start.shape, F32), pltpu.VMEM(noise.shape, BF),
         pltpu.VMEM(time_weight.shape, BF), pltpu.VMEM(w_query.shape, BF), pltpu.VMEM(w_keyval.shape, BF),
         pltpu.VMEM(w_attn_out.shape, BF), pltpu.VMEM(w_up.shape, BF), pltpu.VMEM(w_down.shape, BF),
@@ -377,7 +388,7 @@
         pltpu.VMEM((layers, teams, cores, mine, width), BF),
         pltpu.VMEM((h, rows, width), BF), pltpu.VMEM((h, rows, width), BF),
         pltpu.VMEM((rows, width), F32), pltpu.VMEM((peers, rows, width), F32),
-        dma((5 + 5 * layers,)), dma((h,)), dma((h,)), dma((peers,)), dma((peers,)), dma((1,)), dma((1,)),
+        dma((10 + 5 * layers,)), dma((h,)), dma((h,)), dma((peers,)), dma((peers,)), dma((1,)), dma((1,)),
         dma((layers, teamed)), dma((layers, teamed)), dma((layers, peers)), dma((layers, peers)),
         dma((layers, teamed, peers)), dma((layers, teamed, peers)),
         dma((h,)), dma((h,)), dma((peers,)), dma((peers,)),
@@ -385,15 +396,15 @@
     return pl.pallas_call(
         functools.partial(kernel, sizes),
         out_shape=jax.ShapeDtypeStruct(chain.shape, F32),
-        in_specs=[any_spec] * 3 + [smem] * 3 + [any_spec] * 6 + [vmem] * 2 + [any_spec],
+        in_specs=[hbm] * 15,
         out_specs=vmem,
         scratch_shapes=scratch,
         compiler_params=pltpu.CompilerParams(
-            collective_id=0, has_side_effects=True, vmem_limit_bytes=48 * 1024 * 1024
+            collective_id=0, has_side_effects=True, vmem_limit_bytes=60 * 1024 * 1024
         ),
     )(
         chain, start, noise, timesteps, rates, noise_scales, time_weight, w_query, w_keyval, w_attn_out,
-        w_up, w_down, gains.reshape(-1, width), final_gain.reshape(1, width), w_output,
+        w_up, w_down, gains, final_gain, w_output,
     )
 
 

time: 44.4 us -> 32.3 us (0.73)
  local copies, waits for them, and re-layouts: 12.9 us -> 1.67 us
  Pallas kernels: 31 us -> 30.5 us
    unnamed x25 -> x1, local copies, waits for them, and re-layouts: 12.2 us -> 1.67 us
    reshape x1 -> x0, local copies, waits for them, and re-layouts: 0.71 us -> none  [local(): gains.reshape(-1, width)]
    pallas_call x1, Pallas kernels: 31 us -> 30.5 us  [local(): pl.pallas_call(functools.partial(kernel, sizes), out_shape=jax.ShapeDtype...]
where the time goes in v2:
time: 32.3 us; the launch traced here: 32.2 us
  Pallas kernels  30.5 us (94%)
  local copies, waits for them, and re-layouts  1.67 us (5%)
    pallas_call x1, Pallas kernels, local(): pl.pallas_call(functools.partial(kernel, sizes), out_shape=jax.ShapeDtype...  30.5 us
    unnamed x1, local copies, waits for them, and re-layouts  1.67 us

profile of v2, /device:TPU:0, one launch (start us, length us, event | category | flops | bytes accessed | tf_op | source)
XLA Modules:
  0.0 32.2 jit_solution(2566462450087325897)
XLA Ops:
  0.0 30.5 %shard_map.145 = f32[2,16,4,512]{3,2,1,0:T(4,128)} custom-call(f32[2,16,4,512]{3,2,1,0:T(4,128)} %chain_ref.1, f32[16,4,512]{2,1,0:T(4,128)} %start_ref.1, bf16[2,16,4,512]{3,2,1,0:T(4,128)(2,1)} %noise_ref.1, s32[2]{0:T(128)} %times_hbm.1, f32[2]{0:T(128)} %rates_hbm.1, f32[2]{0:T(128)} %scales_hbm.1, bf16[512,512]{1,0:T(8,128)(2,1)} %tw_ref.1, ...), custom_call_target="tpu_custom_call" | custom-call | tf_op jit(solution)/shard_map/pallas_call | solution.py:396
  30.5 1.7 %copy.17 = f32[2,16,4,512]{3,2,1,0:T(4,128)} copy(f32[2,16,4,512]{3,2,1,0:T(4,128)} %shard_map.145) | data formatting | bytes 524288

commit v3 on v2

--- a/solution.py
+++ b/solution.py
@@ -28,8 +28,8 @@
     tw_ref, wq_ref, wkv_ref, wo_ref, wu_ref, wd_ref, gains_hbm, fgain_hbm, wout_ref,
     out_ref,
     times_ref, rates_ref, scales_ref, gains_ref, fgain_ref, chain_v, start_v, noise_v, tw_v, wq_v, wkv_v, wo_v, wu_v, wd_v, wout_v,
-    send_v, recv_v, temb_v, prev_v, gath, pout, pin, tot_out, tot_in,
-    load_sem, ssend, srecv, tsend, trecv, vsend, vrecv, gsend, grecv, nsend, nrecv, fsend, frecv,
+    send_v, rows_v, temb_v, prev_v, gath, hid_v, stack_v, keyval_v, sum_v, den_v, att_v, pout, pin, tot_out, tot_in,
+    load_sem, ssend, srecv, tsend, trecv, vsend, vrecv, ysend, yrecv, nsend, nrecv,
     rsend, rrecv, usend, urecv,
 ):
     n, cores, h, rows, width, layers = sizes
@@ -101,7 +101,7 @@
         position = (me_s * h + t + 1) % window
         to_p, to_s, slot = position * teams + j, spot // h, spot % h
         own = (to_p == me_p) & (to_s == me_s)
-        copy = remote(send_v.at[t], recv_v.at[slot], ssend.at[t], srecv.at[slot], to_p, to_s)
+        copy = remote(send_v.at[t], rows_v.at[0, slot], ssend.at[t], srecv.at[slot], to_p, to_s)
         scatter.append((own, copy))
 
         @pl.when(jnp.logical_not(own))
@@ -110,7 +110,7 @@
 
         @pl.when(own)
         def _():
-            recv_v[slot] = send_v[t]
+            rows_v[0, slot] = send_v[t]
 
     hand = remote(chain_v.at[h - 1], prev_v, vsend.at[0], vrecv.at[0], me_p, (me_s + 1) % cores)
 
@@ -139,134 +139,163 @@
         )
         share.start()
         shares.append(share)
+    sends = []
+    from_s = ((spot + window - 1) % window) // h
+    for b in range(h):
+        own = (me_s * h + b == spot) & (from_s == me_s)
+
+        @pl.when(jnp.logical_not(own))
+        def _():
+            remote(
+                rows_v.at[0, b], rows_v.at[0, b], ssend.at[0], srecv.at[b], me_p, (me_s + 1) % cores
+            ).wait_recv()
+
+        for d in range(1, teams):
+            copy = remote(
+                rows_v.at[0, b], rows_v.at[d, b], ysend.at[d - 1, b], yrecv.at[d - 1, b],
+                spot * teams + (j + d) % teams, me_s,
+            )
+            copy.start()
+            sends.append(copy)
+
     for d in range(1, cores):
         other = (me_s + cores - d) % cores
         remote(temb_v.at[other], temb_v.at[other], tsend.at[d - 1], trecv.at[d - 1], me_p, other).wait_recv()
     time_row = temb_v[spot // h, pl.ds(spot % h, 1), :]
 
-    from_s = ((spot + window - 1) % window) // h
-    for b in range(h):
-        own = (me_s * h + b == spot) & (from_s == me_s)
-
-        @pl.when(jnp.logical_not(own))
-        def _():
-            remote(
-                recv_v.at[b], recv_v.at[b], ssend.at[0], srecv.at[b], me_p, (me_s + 1) % cores
-            ).wait_recv()
-
-    hidden = recv_v[...].reshape(mine, width).astype(F32) + time_row
-
     head_dim = width // HEADS
     wide = min(256, width)
     per = wide // head_dim
     groups = width // wide
-    lane_head = lax.broadcasted_iota(jnp.int32, (mine, wide), 1) // head_dim
-    masks = [lane_head == i for i in range(per)]
+    masks = [lax.broadcasted_iota(jnp.int32, (mine, wide), 1) // head_dim == i for i in range(per)]
     inner = 1.0 / (math.sqrt(head_dim) * 30.0)
     outer = 30.0 * math.log2(math.e)
-    sends = []
+
+    def each(low, high, act):
+        if high - low <= 2:
+            for r in range(low, high):
+                act(r)
+        else:
+
+            @pl.loop(low, high)
+            def _(r):
+                act(r)
+
+    def share(l, r, e):
+        return remote(
+            gath.at[l, 0, r], gath.at[l, e, r], nsend.at[l, e - 1, r], nrecv.at[l, e - 1, r],
+            me_p, (me_s + e) % cores,
+        )
+
+    def arrive(r):
+        for b in range(h):
+            remote(
+                rows_v.at[r, b], rows_v.at[r, b], ysend.at[r - 1, b], yrecv.at[r - 1, b],
+                me_p, (me_s + 1) % cores,
+            ).wait_recv()
+
+    def begin(r):
+        hid_v[r] = rows_v[r].reshape(mine, width).astype(F32) + time_row
+
+    def normalize(l, r):
+        gath[l, 0, r] = rms_norm(hid_v[r], gains_ref[l, 0:1, :]).astype(BF)
+        for e in range(1, cores):
+            share(l, r, e).start()
+
+    def query(l, r):
+        queries = dot(gath[l, 0, r], wq_v[l]).astype(BF)
+        for g in range(groups):
+            piece = queries[:, g * wide : (g + 1) * wide]
+            for i in range(per):
+                stack_v[r, g, i * mine : (i + 1) * mine, :] = jnp.where(masks[i], piece, jnp.zeros_like(piece))
+
+    def keys_of(l, r):
+        for e in range(1, cores):
+            share(l, r, e).wait_recv()
+        keyval_v[r] = dot(gath[l, :, r].reshape(cores * mine, width), wkv_v[l]).astype(BF)
+
+    def attend(r, k, fresh):
+        for g in range(groups):
+            keys = keyval_v[k, :, g * wide : (g + 1) * wide]
+            values = keyval_v[k, :, width + g * wide : width + (g + 1) * wide]
+            scores = lax.dot_general(
+                stack_v[r, g], keys, (((1,), (1,)), ((), ())), preferred_element_type=F32
+            )
+            expo = jnp.exp2(jnp.tanh(scores * inner) * outer)
+            part = dot(expo.astype(BF), values)
+            total = part[:mine]
+            for i in range(1, per):
+                total = jnp.where(masks[i], part[i * mine : (i + 1) * mine], total)
+            den = expo[:, :128]
+            for c in range(128, cores * mine, 128):
+                den = den + expo[:, c : c + 128]
+            if fresh:
+                sum_v[r, g] = total
+                den_v[r, g] = den
+            else:
+                sum_v[r, g] = sum_v[r, g] + total
+                den_v[r, g] = den_v[r, g] + den
+
+    def finish(r):
+        for g in range(groups):
+            inverse = 1.0 / jnp.sum(den_v[r, g], axis=-1, keepdims=True)
+            scale = jnp.broadcast_to(inverse[:mine], (mine, wide))
+            for i in range(1, per):
+                scale = jnp.where(masks[i], inverse[i * mine : (i + 1) * mine], scale)
+            att_v[r, :, g * wide : (g + 1) * wide] = (sum_v[r, g] * scale).astype(BF)
+
+    def feed(l, r, count):
+        part = pl.ds(r, count)
+        hidden = hid_v[part].reshape(count * mine, width)
+        hidden = hidden + dot(att_v[part].reshape(count * mine, width), wo_v[l])
+        mixed = rms_norm(hidden, gains_ref[l, 1:2, :]).astype(BF)
+        upward = jax.nn.gelu(dot(mixed, wu_v[l])).astype(BF)
+        hidden = hidden + dot(upward, wd_v[l])
+        hid_v[part] = hidden.reshape(count, mine, width)
 
     loads["gains"].wait()
     for l in range(layers):
-        normed = rms_norm(hidden, gains_ref[l, 0:1, :]).astype(BF)
-        gath[l, j, me_s] = normed
-        own_block = gath.at[l, j, me_s]
-        for d in range(1, teams):
-            copy = remote(
-                own_block, own_block, gsend.at[l, d - 1], grecv.at[l, d - 1],
-                spot * teams + (j + d) % teams, me_s,
-            )
-            copy.start()
-            sends.append(copy)
-        for e in range(1, cores):
-            copy = remote(
-                own_block, own_block, nsend.at[l, e - 1], nrecv.at[l, e - 1], me_p, (me_s + e) % cores
-            )
-            copy.start()
-            sends.append(copy)
+        active = teams if l < layers - 1 else 1
+        if l == 0:
+            begin(0)
+            normalize(l, 0)
+        else:
+            each(0, teams, lambda r: normalize(l, r))
         loads["wq", l].wait()
-        queries = dot(normed, wq_v[l]).astype(BF)
-        stacked = []
-        for g in range(groups):
-            piece = queries[:, g * wide : (g + 1) * wide]
-            stacked.append(jnp.concatenate([jnp.where(m, piece, jnp.zeros_like(piece)) for m in masks], axis=0))
+        query(l, 0)
         loads["wkv", l].wait()
-
-        def round_of(team, carry, l=l, stacked=stacked):
-            sums, dens = carry
-            keyval = dot(gath[l, team].reshape(cores * mine, width), wkv_v[l]).astype(BF)
-            new_sums, new_dens = [], []
-            for g in range(groups):
-                keys = keyval[:, g * wide : (g + 1) * wide]
-                values = keyval[:, width + g * wide : width + (g + 1) * wide]
-                scores = lax.dot_general(
-                    stacked[g], keys, (((1,), (1,)), ((), ())), preferred_element_type=F32
-                )
-                expo = jnp.exp2(jnp.tanh(scores * inner) * outer)
-                part = dot(expo.astype(BF), values)
-                total = sums[g]
-                for i in range(per):
-                    total = total + jnp.where(masks[i], part[i * mine : (i + 1) * mine], 0.0)
-                new_sums.append(total)
-                den = dens[g]
-                for c in range(0, cores * mine, 128):
-                    den = den + expo[:, c : c + 128]
-                new_dens.append(den)
-            return tuple(new_sums), tuple(new_dens)
-
-        carry = (
-            tuple(jnp.zeros((mine, wide), F32) for _ in range(groups)),
-            tuple(jnp.zeros((per * mine, 128), F32) for _ in range(groups)),
-        )
-        for e in range(1, cores):
-            other = gath.at[l, j, (me_s + cores - e) % cores]
-            remote(
-                other, other, nsend.at[l, e - 1], nrecv.at[l, e - 1], me_p, (me_s + e) % cores
-            ).wait_recv()
-        carry = round_of(j, carry)
-        for d in range(1, teams):
-            team = (j + teams - d) % teams
-            block = gath.at[l, team, me_s]
-            remote(
-                block, block, gsend.at[l, d - 1], grecv.at[l, d - 1], spot * teams + team, me_s
-            ).wait_recv()
-            for e in range(1, cores):
-                copy = remote(
-                    block, block, fsend.at[l, d - 1, e - 1], frecv.at[l, d - 1, e - 1],
-                    me_p, (me_s + e) % cores,
-                )
-                copy.start()
-                sends.append(copy)
-        for d in range(1, teams):
-            team = (j + teams - d) % teams
-            for e in range(1, cores):
-                block = gath.at[l, team, (me_s + cores - e) % cores]
-                remote(
-                    block, block, fsend.at[l, d - 1, e - 1], frecv.at[l, d - 1, e - 1],
-                    me_p, (me_s + e) % cores,
-                ).wait_recv()
-        if teams <= 2:
-            for d in range(1, teams):
-                carry = round_of((j + teams - d) % teams, carry)
+        keys_of(l, 0)
+        attend(0, 0, True)
+        if l == 0:
+
+            def enter(r):
+                arrive(r)
+                begin(r)
+                normalize(l, r)
+
+            each(1, teams, enter)
+
+        def follow(r):
+            query(l, r)
+            attend(r, 0, True)
+
+        each(1, active, follow)
+
+        def sweep(k):
+            keys_of(l, k)
+            each(0, active, lambda r: attend(r, k, False))
+
+        each(1, teams, sweep)
+        each(0, active, finish)
+        loads["wo", l].wait()
+        loads["wu", l].wait()
+        loads["wd", l].wait()
+        if active <= 2:
+            feed(l, 0, active)
         else:
-            carry = lax.fori_loop(1, teams, lambda d, c: round_of((j + teams - d) % teams, c), carry)
-        sums, dens = carry
-        pieces = []
-        for g in range(groups):
-            inverse = 1.0 / jnp.sum(dens[g], axis=-1, keepdims=True)
-            scale = jnp.zeros((mine, wide), F32)
-            for i in range(per):
-                scale = jnp.where(masks[i], inverse[i * mine : (i + 1) * mine], scale)
-            pieces.append((sums[g] * scale).astype(BF))
-        attended = jnp.concatenate(pieces, axis=1)
-        loads["wo", l].wait()
-        hidden = hidden + dot(attended, wo_v[l])
-        mixed = rms_norm(hidden, gains_ref[l, 1:2, :]).astype(BF)
-        loads["wu", l].wait()
-        upward = jax.nn.gelu(dot(mixed, wu_v[l])).astype(BF)
-        loads["wd", l].wait()
-        hidden = hidden + dot(upward, wd_v[l])
-
+            each(0, active, lambda r: feed(l, r, 1))
+
+    hidden = hid_v[0]
     loads["fgain"].wait()
     final_rows = rms_norm(hidden, fgain_ref[...].reshape(1, width)).astype(BF)
     loads["wout"].wait()
@@ -357,6 +386,9 @@
 
     for copy in shares + sends:
         copy.wait_send()
+    for l in range(layers):
+        for e in range(1, cores):
+            each(0, teams, lambda r: share(l, r, e).wait_send())
     for d, up in enumerate(ups):
 
         @pl.when(me_s + d + 1 < cores)
@@ -375,6 +407,8 @@
     hbm = pl.BlockSpec(memory_space=pltpu.HBM)
     vmem = pl.BlockSpec(memory_space=pltpu.VMEM)
     dma = pltpu.SemaphoreType.DMA
+    wide = min(256, width)
+    per, groups = wide * HEADS // width, width // wide
     peers, teamed = max(cores - 1, 1), max(teams - 1, 1)
     scratch = [
         pltpu.SMEM(timesteps.shape, jnp.int32), pltpu.SMEM(rates.shape, F32), pltpu.SMEM(rates.shape, F32),
@@ -383,14 +417,16 @@
         pltpu.VMEM(time_weight.shape, BF), pltpu.VMEM(w_query.shape, BF), pltpu.VMEM(w_keyval.shape, BF),
         pltpu.VMEM(w_attn_out.shape, BF), pltpu.VMEM(w_up.shape, BF), pltpu.VMEM(w_down.shape, BF),
         pltpu.VMEM(w_output.shape, BF),
-        pltpu.VMEM((h, rows, width), BF), pltpu.VMEM((h, rows, width), BF),
+        pltpu.VMEM((h, rows, width), BF), pltpu.VMEM((teams, h, rows, width), BF),
         pltpu.VMEM((cores, 8, width), F32), pltpu.VMEM(start.shape, F32),
-        pltpu.VMEM((layers, teams, cores, mine, width), BF),
+        pltpu.VMEM((layers, cores, teams, mine, width), BF), pltpu.VMEM((teams, mine, width), F32),
+        pltpu.VMEM((teams, groups, per * mine, wide), BF), pltpu.VMEM((teams, cores * mine, 2 * width), BF),
+        pltpu.VMEM((teams, groups, mine, wide), F32), pltpu.VMEM((teams, groups, per * mine, 128), F32),
+        pltpu.VMEM((teams, mine, width), BF),
         pltpu.VMEM((h, rows, width), BF), pltpu.VMEM((h, rows, width), BF),
         pltpu.VMEM((rows, width), F32), pltpu.VMEM((peers, rows, width), F32),
         dma((10 + 5 * layers,)), dma((h,)), dma((h,)), dma((peers,)), dma((peers,)), dma((1,)), dma((1,)),
-        dma((layers, teamed)), dma((layers, teamed)), dma((layers, peers)), dma((layers, peers)),
-        dma((layers, teamed, peers)), dma((layers, teamed, peers)),
+        dma((teamed, h)), dma((teamed, h)), dma((layers, peers, teams)), dma((layers, peers, teams)),
         dma((h,)), dma((h,)), dma((peers,)), dma((peers,)),
     ]
     return pl.pallas_call(

time: 32.3 us -> 29.8 us (0.923)
  Pallas kernels: 30.5 us -> 28 us
    pallas_call x1, Pallas kernels: 30.5 us -> 28 us  [local(): pl.pallas_call(functools.partial(kernel, sizes), out_shape=jax.ShapeDtype...]
where the time goes in v3:
time: 29.8 us; the launch traced here: 29.7 us
  Pallas kernels  28 us (94%)
  local copies, waits for them, and re-layouts  1.67 us (6%)
    pallas_call x1, Pallas kernels, local(): pl.pallas_call(functools.partial(kernel, sizes), out_shape=jax.ShapeDtype...  28 us
    unnamed x1, local copies, waits for them, and re-layouts  1.67 us

profile of v3, /device:TPU:0, one launch (start us, length us, event | category | flops | bytes accessed | tf_op | source)
XLA Modules:
  0.0 29.7 jit_solution(9801949989366949396)
XLA Ops:
  0.0 28.0 %shard_map.145 = f32[2,16,4,512]{3,2,1,0:T(4,128)} custom-call(f32[2,16,4,512]{3,2,1,0:T(4,128)} %chain_ref.1, f32[16,4,512]{2,1,0:T(4,128)} %start_ref.1, bf16[2,16,4,512]{3,2,1,0:T(4,128)(2,1)} %noise_ref.1, s32[2]{0:T(128)} %times_hbm.1, f32[2]{0:T(128)} %rates_hbm.1, f32[2]{0:T(128)} %scales_hbm.1, bf16[512,512]{1,0:T(8,128)(2,1)} %tw_ref.1, ...), custom_call_target="tpu_custom_call" | custom-call | tf_op jit(solution)/shard_map/pallas_call | solution.py:432
  28.0 1.7 %copy.17 = f32[2,16,4,512]{3,2,1,0:T(4,128)} copy(f32[2,16,4,512]{3,2,1,0:T(4,128)} %shard_map.145) | data formatting | bytes 524288

commit v4 on v3

--- a/solution.py
+++ b/solution.py
@@ -429,6 +429,13 @@
         dma((teamed, h)), dma((teamed, h)), dma((layers, peers, teams)), dma((layers, peers, teams)),
         dma((h,)), dma((h,)), dma((peers,)), dma((peers,)),
     ]
+    chain, start, noise, timesteps, rates, noise_scales, time_weight, w_query, w_keyval, w_attn_out, w_up, w_down, gains, final_gain, w_output = (
+        pltpu.with_memory_space_constraint(array, pltpu.HBM)
+        for array in (
+            chain, start, noise, timesteps, rates, noise_scales, time_weight, w_query, w_keyval, w_attn_out, w_up,
+            w_down, gains, final_gain, w_output,
+        )
+    )
     return pl.pallas_call(
         functools.partial(kernel, sizes),
         out_shape=jax.ShapeDtypeStruct(chain.shape, F32),
@@ -436,7 +443,7 @@
         out_specs=vmem,
         scratch_shapes=scratch,
         compiler_params=pltpu.CompilerParams(
-            collective_id=0, has_side_effects=True, vmem_limit_bytes=60 * 1024 * 1024
+            collective_id=0, has_side_effects=True, vmem_limit_bytes=48 * 1024 * 1024
         ),
     )(
         chain, start, noise, timesteps, rates, noise_scales, time_weight, w_query, w_keyval, w_attn_out,

time: 29.8 us -> 28.1 us (0.943)
  local copies, waits for them, and re-layouts: 1.67 us -> 0.71 us
  Pallas kernels: 28 us -> 27.3 us
    unnamed x1, local copies, waits for them, and re-layouts: 1.67 us -> 0.71 us
    pallas_call x1, Pallas kernels: 28 us -> 27.3 us  [local(): pl.pallas_call(functools.partial(kernel, sizes), out_shape=jax.ShapeDtype...]
where the time goes in v4:
time: 28.1 us; the launch traced here: 28 us
  Pallas kernels  27.3 us (97%)
  local copies, waits for them, and re-layouts  0.71 us (3%)
    pallas_call x1, Pallas kernels, local(): pl.pallas_call(functools.partial(kernel, sizes), out_shape=jax.ShapeDtype...  27.3 us
    unnamed x1, local copies, waits for them, and re-layouts  0.71 us

profile of v4, /device:TPU:0, one launch (start us, length us, event | category | flops | bytes accessed | tf_op | source)
XLA Modules:
  0.0 28.0 jit_solution(4719515297057620039)
XLA Ops:
  0.0 27.3 %shard_map.145 = f32[2,16,4,512]{3,2,1,0:T(4,128)S(1)} custom-call(f32[2,16,4,512]{3,2,1,0:T(4,128)} %chain_ref.1, f32[16,4,512]{2,1,0:T(4,128)} %start_ref.1, bf16[2,16,4,512]{3,2,1,0:T(4,128)(2,1)} %noise_ref.1, s32[2]{0:T(128)} %times_hbm.1, f32[2]{0:T(128)} %rates_hbm.1, f32[2]{0:T(128)} %scales_hbm.1, bf16[512,512]{1,0:T(8,128)(2,1)} %tw_ref.1, ...), custom_call_target="tpu_custom_call" | custom-call | tf_op jit(solution)/shard_map/pallas_call | solution.py:439
  27.3 0.7 %copy.17 = f32[2,16,4,512]{3,2,1,0:T(4,128)} copy(f32[2,16,4,512]{3,2,1,0:T(4,128)S(1)} %shard_map.145) | data formatting | bytes 524288
